TPU v7x, 32 devices: a whole 2x2x4 slice. The times are simulated.
32 devices in a mesh: group: 2 (over y), ctx: 4 (over z), head: 4 (over x, core).
Axes of the slice: x: 2, y: 2, z: 4, core: 2. Of those that a mesh axis runs over, the one named last changes fastest.
Arguments:
- head_input: bfloat16 [4096, 8192], P(('group', 'ctx'), 'head'), parts along dimension 0, may hold values from -6 to 6
- gate_input: bfloat16 [4096, 8192], P(('group', 'ctx'), 'head'), parts along dimension 0, may hold values from -40 to 40
- input_map: bfloat16 [4096, 2048], P(('group', 'ctx'), 'head'), parts along dimension 0, may hold values from -4 to 4
- output_map: bfloat16 [4096, 2048], P(('group', 'ctx'), 'head'), parts along dimension 0, may hold values from -4 to 4
- step_size: float32 [128, 4096], P('head', ('group', 'ctx')), parts along dimension 1, may hold values from 0.1 to 0.4
- decays: float32 [128, 4096], P('head', ('group', 'ctx')), parts along dimension 1, may hold values from 0.45 to 1
- bypass_scale: float32 [128], P('head'), may hold values from 1 to 4
- norm_gain: bfloat16 [8192], P('head'), may hold values from 0.099609375 to 1.8984375
- out_weight: bfloat16 [8192, 4096], P('head', 'ctx'), may hold values from -0.0625 to 0.0625
Outputs:
- layer_out: bfloat16 [4096, 4096], P(('group', 'ctx', 'head')), parts along dimension 0
There are 2 independent parts, one for each index of `group`. A program takes and returns all parts, laid end to end along the dimension named above; an argument that names none is the same for every part. Nothing has to cross between parts.
All inputs are finite; a program needn't handle non-finite values.
Results may differ from a plain program's by a relative error of at most 0.014.
Values may be sent and summed in bfloat16 or wider, within the bound.
A program may use at most 128 MiB of HBM per device.

v0:
```python
import jax
import jax.numpy as jnp
from jax import lax
from jax.sharding import PartitionSpec as P

HEADP = 64
STATE = 256
STRETCH = 128


def carried_in(shard, axis, combine, identity):
    size, position = (lax.axis_size(axis), lax.axis_index(axis))
    everything = jax.tree.map(
        lambda part, kind: lax.all_gather(part.astype(kind), axis),
        shard,
        (jnp.bfloat16, jnp.bfloat16),
    )
    start = jax.tree.map(
        lambda part, zero: jnp.broadcast_to(jnp.asarray(zero, part.dtype), part.shape),
        shard,
        identity,
    )

    def lap(k, before):
        reached = k < position
        new = combine(
            before, jax.tree.map(lambda part, own: part[k].astype(own.dtype), everything, shard)
        )
        return jax.tree.map(lambda a, b: jnp.where(reached, a, b), new, before)

    return lax.fori_loop(0, size, lap, start)


def block_term_values(inputs, in_maps, out_maps, steps, decays):
    count, length, groups, per_group, channels = inputs.shape
    ramps = jnp.cumsum(jnp.log(decays), axis=-1)
    rows = lax.broadcasted_iota(jnp.int32, (length, length), 0)
    cols = lax.broadcasted_iota(jnp.int32, (length, length), 1)
    lower = rows >= cols
    spread = ramps[:, :, :, None] - ramps[:, :, None, :]
    within_decay = jnp.where(lower, jnp.exp(jnp.where(lower, spread, 0.0)), 0.0)
    scores = jnp.einsum("kqgn,ksgn->kgqs", out_maps, in_maps, preferred_element_type=jnp.float32)
    mixing = within_decay.reshape(count, groups, per_group, length, length) * scores[:, :, None]
    mixing = mixing * steps.reshape(count, groups, per_group, 1, length)
    mixing = mixing.astype(jnp.bfloat16)
    within = jnp.einsum("kgjqs,ksgjp->kqgjp", mixing, inputs, preferred_element_type=jnp.float32)
    tails = jnp.exp(ramps[:, :, -1:] - ramps) * steps
    tails = jnp.transpose(tails.reshape(count, groups, per_group, length), (0, 3, 1, 2))[..., None]
    weighted = (inputs.astype(jnp.float32) * tails).astype(jnp.bfloat16)
    block_state = jnp.einsum(
        "ksgjp,ksgn->kgjpn", weighted, in_maps, preferred_element_type=jnp.float32
    )
    accumulated_sums_list = jnp.exp(ramps[:, :, -1]).reshape(count, groups, per_group)
    entry = jnp.transpose(jnp.exp(ramps).reshape(count, groups, per_group, length), (0, 3, 1, 2))[
        ..., None
    ]
    return (within, block_state, accumulated_sums_list, entry)


def join_states(earlier, later):
    early_decay, early_state = earlier
    late_decay, late_state = later
    return (early_decay * late_decay, late_decay[..., None, None] * early_state + late_state)


def shards(
    head_input,
    gate_input,
    input_map,
    output_map,
    step_size,
    decays,
    bypass_scale,
    norm_gain,
    out_weight,
):
    tok_rows, width = head_input.shape
    heads = step_size.shape[0]
    groups = input_map.shape[1] // STATE
    per_group = heads // groups
    blocks = tok_rows // STRETCH
    inputs = head_input.reshape(blocks, STRETCH, groups, per_group, HEADP)
    in_maps = input_map.reshape(blocks, STRETCH, groups, STATE)
    out_maps = output_map.reshape(blocks, STRETCH, groups, STATE)
    steps = jnp.transpose(step_size.reshape(heads, blocks, STRETCH), (1, 0, 2))
    rates = jnp.transpose(decays.reshape(heads, blocks, STRETCH), (1, 0, 2))
    within, block_state, accumulated_sums_list, entry = block_term_values(
        inputs, in_maps, out_maps, steps, rates
    )

    def advance(carry, item):
        state, lead = carry
        total, piece = item
        return ((total[..., None, None] * state + piece, total * lead), (state, lead))

    empty_state = jnp.zeros((groups, per_group, HEADP, STATE), jnp.float32)
    unit_decay = jnp.ones((groups, per_group), jnp.float32)
    (local_state, local_decay), (local_entering, leads) = lax.scan(
        advance, (empty_state, unit_decay), (accumulated_sums_list, block_state)
    )
    incoming_decay, incoming = carried_in(
        (local_decay, local_state), "ctx", join_states, (unit_decay, empty_state)
    )
    entering = local_entering + leads[..., None, None] * incoming
    carried = (
        jnp.einsum(
            "kqgn,kgjpn->kqgjp",
            out_maps.astype(jnp.float32),
            entering,
            precision=lax.Precision.HIGHEST,
        )
        * entry
    )
    skip = bypass_scale.reshape(groups, per_group, 1)
    mamba_out = (within + carried + skip * inputs.astype(jnp.float32)).reshape(tok_rows, width)
    gated = mamba_out * jax.nn.silu(gate_input.astype(jnp.float32))
    grouped = gated.reshape(tok_rows, groups, -1)
    factor = lax.rsqrt(jnp.mean(grouped * grouped, axis=-1, keepdims=True) + 1e-05)
    normed = ((grouped * factor).reshape(tok_rows, width) * norm_gain.astype(jnp.float32)).astype(
        jnp.bfloat16
    )
    terms = jnp.dot(
        normed,
        lax.all_gather(out_weight, "ctx", axis=1, tiled=True),
        preferred_element_type=jnp.float32,
    )
    summed = lax.psum_scatter(terms.astype(jnp.bfloat16), "head", scatter_dimension=0, tiled=True)
    return summed


def solution(mesh):
    return jax.shard_map(
        shards,
        mesh=mesh,
        in_specs=(
            P(("group", "ctx"), "head"),
            P(("group", "ctx"), "head"),
            P(("group", "ctx"), "head"),
            P(("group", "ctx"), "head"),
            P("head", ("group", "ctx")),
            P("head", ("group", "ctx")),
            P("head"),
            P("head"),
            P("head", "ctx"),
        ),
        out_specs=P(("group", "ctx", "head"), None),
        check_vma=False,
    )
```

profile of v0, /device:TPU:27, one launch (start us, length us, event | category | flops | bytes accessed | tf_op | source)
XLA Modules:
  0.0 475.5 jit_solution(10169969477722998015)
XLA Ops:
  8.8 7.1 %reshape.83 = bf16[4,128,2,16,64]{4,3,2,1,0:T(8,128)(2,1)} reshape(bf16[512,2048]{1,0:T(8,128)(2,1)} %param.13) | data formatting | bytes 4194304 | tf_op jit(solution)/shard_map/reshape | solution.py:82
  15.9 6.5 %copy.27 = bf16[4,128,2,16,64]{1,4,3,2,0:T(8,128)(2,1)} copy(bf16[4,128,2,16,64]{4,3,2,1,0:T(8,128)(2,1)} %reshape.83) | data formatting | bytes 4194304 | tf_op jit(solution)/shard_map/reshape | solution.py:82
  22.7 6.1 %fusion.23 = f32[4,2,16,64,256]{4,3,2,1,0:T(8,128)} fusion(bf16[4,128,2,16,64]{1,4,3,2,0:T(8,128)(2,1)} %copy.27, f32[4,128,2,16]{1,3,2,0:T(8,128)S(1)} %bitcast.92, bf16[4,128,2,256,1]{3,2,1,0,4:T(2,128)(2,1)S(1)} %bitcast.89), kind=kOutput, calls=%fused_computation.39 | convolution fusion | flops 540016640 | bytes 11075584 | tf_op jit(solution)/shard_map/ksgjp,ksgn->kgjpn/dot_general | solution.py:50
  28.8 14.3 %while.31 = (s32[]{:T(128)}, f32[2,16,64,256]{3,2,1,0:T(8,128)S(1)}, f32[2,16]{1,0:T(2,128)S(1)}, f32[4,2,16,64,256]{4,3,2,1,0:T(8,128)}, f32[4,2,16]{2,1,0:T(2,...) while((s32[]{:T(128)}, ...), condition=%wide.region_2.3_spmd.clone, body=%wide.region_1.2_spmd.clone.sunk | while | flops 2097251 | bytes 10489078 | solution.py:98
  28.8 1.5 bitcast_dynamic-update-slice_fusion.4
  30.3 2.0 bitcast_add_fusion.2
  33.9 2.0 bitcast_add_fusion.2
  37.5 2.0 bitcast_add_fusion.2
  41.0 2.0 bitcast_add_fusion.2
  46.3 3.9 copy.32
  50.3 5.7 %all-gather.2 = bf16[4,2,16]{2,1,0:T(2,128)(2,1)S(1)} all-gather(bf16[1,2,16]{2,1,0:T(2,128)(2,1)S(1)} %convert_bitcast_fusion), channel_id=2, replica_groups=mesh['group'=2,'ctx'=4,'head'=4] {'ctx'}, dimensions={0}, use_global_device_ids=true | all-gather | bytes 320 | tf_op jit(solution)/shard_map/all_gather | solution.py:14
  57.2 66.7 %all-gather.8.cloned.1.call-done = bf16[8,16,64,256]{3,2,1,0:T(8,128)(2,1)} async-done(((bf16[2,16,64,256]{3,2,1,0:T(8,128)(2,1)}), bf16[8,16,64,256]{3,2,1,0:T(8,128)(2,1)}) %all-gather.8.cloned.1.call-update) | async-done | bytes 4194320 | tf_op jit(solution)/shard_map/all_gather | solution.py:14
  123.8 9.0 %while.32 = (s32[]{:T(128)}, f32[2,16,64,256]{3,2,1,0:T(8,128)S(1)}, s32[]{:T(128)}, bf16[4,2,16]{2,1,0:T(2,128)(2,1)S(1)}, bf16[4,2,16,64,256]{4,3,2,1,0:T(8,128)(2,1)}, /*index=5*/s32[]{:T(128)}, s32[]{:T(128)}) while((s32[]{:T(128)}, f32[2,16,64,256]{3,2,1,0:T(8,128)S(1)}, s32[]{:T(128)}, bf16[4,2,16]{2,1,0:T(2,128)(2,1)S(1)}, ...), condition=%wide.region_4.5_spmd.clone, body=%wide.region_3.4_spmd.clone.sunk | while | flops 2621476 | bytes 5243305 | solution.py:31
  123.8 2.2 fusion.40
  126.1 2.2 fusion.40
  128.4 2.2 fusion.40
  130.6 2.2 fusion.40
  132.9 7.8 %fusion.2 = f32[4,2,16,64,128]{4,3,2,1,0:T(8,128)S(1)} fusion(f32[4,2,16,64,256]{4,3,2,1,0:T(8,128)} %get-tuple-element.139, f32[2,16,64,256]{3,2,1,0:T(8,128)S(1)} %get-tuple-element.143, f32[4,2,16]{2,1,0:T(2,128)S(1)} %get-tuple-element.140, bf16[4,128,2,256,1]{3,2,1,0,4:T(2,128)(2,1)S(1)} %bitcast.88), kind=kOutput, calls=%fused_computation.9 | convolution fusion | flops 3225419776 | bytes 15204864 | tf_op jit(solution)/shard_map/kqgn,kgjpn->kqgjp/dot_general | solution.py:106
  140.8 3.6 fusion.7
  144.4 3.6 copy.31
  149.4 1.7 fusion.13
  151.2 259.3 %all-gather.6.cloned.1.call-done = bf16[2048,4096]{1,0:T(8,128)(2,1)} async-done(((bf16[2048,1024]{1,0:T(8,128)(2,1)}), bf16[2048,4096]{1,0:T(8,128)(2,1)}) %all-gather.6.cloned.1.call-update) | async-done | bytes 16777232 | tf_op jit(solution)/shard_map/all_gather | solution.py:124
  410.4 14.0 %convolution_convert_fusion = bf16[512,4096]{1,0:T(8,128)(2,1)} fusion(bf16[512,2048]{0,1:T(8,128)(2,1)S(1)} %fusion.13, bf16[2048,4096]{1,0:T(8,128)(2,1)} %all-gather.6.cloned.1.call-done), kind=kOutput, calls=%fused_computation.13 | convolution fusion | flops 8592031744 | bytes 23068672 | tf_op jit(solution)/shard_map/dot_general | solution.py:122
  424.4 44.5 %reduce-scatter.2.cloned.1.call-done = bf16[128,4096]{1,0:T(8,128)(2,1)} async-done(((bf16[512,4096]{1,0:T(8,128)(2,1)}), bf16[128,4096]{1,0:T(8,128)(2,1)}) %reduce-scatter.2.cloned.1.call-update) | async-done | bytes 1048592 | tf_op jit(solution)/shard_map/reduce_scatter | solution.py:127
  (59 shorter events, 12.9 us)
Async XLA Ops:
  6.5 16.1 %copy-start = (f32[32,512]{1,0:T(8,128)S(1)}, f32[32,512]{1,0:T(8,128)}, u32[]{:S(2)}) copy-start(f32[32,512]{1,0:T(8,128)} %param.17) | copy-start | bytes 196612
  6.5 117.3 %all-gather.8.cloned.1.call-start = ((), (), s32[]{:S(2)}) async-start(), calls=%async_computation.3 | async-start | bytes 5242880 | tf_op jit(solution)/shard_map/all_gather | solution.py:14
  15.9 6.5 %copy-start.5 = (bf16[512,512]{1,0:T(8,128)(2,1)S(1)}, bf16[512,512]{1,0:T(8,128)(2,1)}, u32[]{:S(2)}) copy-start(bf16[512,512]{1,0:T(8,128)(2,1)} %param.15) | copy-start | bytes 1572868
  43.1 3.2 copy-start.7
  44.2 6.0 %copy-start.6 = (bf16[2048]{0:T(1024)(128)(2,1)S(1)}, bf16[2048]{0:T(1024)(128)(2,1)}, u32[]{:S(2)}) copy-start(bf16[2048]{0:T(1024)(128)(2,1)} %param.20) | copy-start | bytes 12292
  44.2 366.2 %all-gather.6.cloned.1.call-start = ((), (), s32[]{:S(2)}) async-start(), calls=%async_computation.1 | async-start | bytes 20971520 | tf_op jit(solution)/shard_map/all_gather | solution.py:124
  45.0 424.0 %reduce-scatter.2.cloned.1.call-start = ((), (), s32[]{:S(2)}) async-start(), calls=%async_computation.2 | async-start | bytes 5242880 | tf_op jit(solution)/shard_map/reduce_scatter | solution.py:127
  132.9 7.9 %copy-start.3 = (bf16[4,128,2,16,64]{1,4,3,2,0:T(8,128)(2,1)S(1)}, bf16[4,128,2,16,64]{1,4,3,2,0:T(8,128)(2,1)}, u32[]{:S(2)}) copy-start(bf16[4,128,2,16,64]{1,4,3,2,0:T(8,128)(2,1)} %copy.27) | copy-start | bytes 6291460
  132.9 7.9 %copy-start.4 = (f32[4,2,128,128]{3,2,1,0:T(8,128)S(1)}, f32[4,2,128,128]{3,2,1,0:T(8,128)}, u32[]{:S(2)}) copy-start(f32[4,2,128,128]{3,2,1,0:T(8,128)} %fusion.28) | copy-start | bytes 1572868
  144.4 3.6 copy-start.2
  410.4 58.6 %copy-start.1 = (f32[32,512]{1,0:T(8,128)S(1)}, f32[32,512]{1,0:T(8,128)}, u32[]{:S(2)}) copy-start(f32[32,512]{1,0:T(8,128)} %param.17) | copy-start | bytes 196612
Sparse Core Ops, SparseCore 0:
  44.4 79.4 all-gather.7
  125.4 284.9 all-gather.5
  424.5 44.3 reduce-scatter.1
where the time goes:
time: 479 us; the launch traced here: 476 us
  waiting for transfers between devices  371 us (77%)
  matrix products  32.6 us (7%)
  other arithmetic  28.6 us (6%)
  local copies, waits for them, and re-layouts  23.7 us (5%)
  between operations  13.3 us (3%)
  blocking collectives  5.74 us (1%)
    all_gather x1, waiting for transfers between devices, shards(): lax.all_gather(out_weight, 'ctx', axis=1, tiled=True)  259 us
    all_gather x1, waiting for transfers between devices, carried_in(): lax.all_gather(part.astype(kind), axis)  66.7 us
    reduce_scatter x1, waiting for transfers between devices, shards(): lax.psum_scatter(terms.astype(jnp.bfloat16), 'head', scatter_dimension=0,...  44.5 us
    dot_general x1, matrix products, shards(): jnp.dot(normed, lax.all_gather(out_weight, 'ctx', axis=1, tiled=True), pr...  14 us
    reshape x2, local copies, waits for them, and re-layouts, shards(): inputs = head_input.reshape(blocks, STRETCH, groups, per_group, HEADP)  13.6 us
  transfers between devices with their start and end apart: 3, of which 3 were waited for; matrix products, arithmetic and copies ran while one was open for 7% of the time, Pallas kernels for 0%

commit v1 on v0

--- a/solution.py
+++ b/solution.py
@@ -8,27 +8,15 @@
 STRETCH = 128
 
 
-def carried_in(shard, axis, combine, identity):
-    size, position = (lax.axis_size(axis), lax.axis_index(axis))
-    everything = jax.tree.map(
-        lambda part, kind: lax.all_gather(part.astype(kind), axis),
-        shard,
-        (jnp.bfloat16, jnp.bfloat16),
-    )
-    start = jax.tree.map(
-        lambda part, zero: jnp.broadcast_to(jnp.asarray(zero, part.dtype), part.shape),
-        shard,
-        identity,
-    )
-
-    def lap(k, before):
-        reached = k < position
-        new = combine(
-            before, jax.tree.map(lambda part, own: part[k].astype(own.dtype), everything, shard)
-        )
-        return jax.tree.map(lambda a, b: jnp.where(reached, a, b), new, before)
-
-    return lax.fori_loop(0, size, lap, start)
+def carried_in(shard, axis):
+    size, position = lax.axis_size(axis), lax.axis_index(axis)
+    decay, state = shard
+    hops = [(i, i + 1) for i in range(size - 1)]
+    incoming = jnp.zeros_like(state)
+    for hop in range(size - 1):
+        total = (decay[..., None, None] * incoming + state).astype(jnp.bfloat16)
+        incoming = lax.ppermute(total, axis, hops).astype(jnp.float32)
+    return incoming
 
 
 def block_term_values(inputs, in_maps, out_maps, steps, decays):
@@ -55,12 +43,6 @@
         ..., None
     ]
     return (within, block_state, accumulated_sums_list, entry)
-
-
-def join_states(earlier, later):
-    early_decay, early_state = earlier
-    late_decay, late_state = later
-    return (early_decay * late_decay, late_decay[..., None, None] * early_state + late_state)
 
 
 def shards(
@@ -98,9 +80,7 @@
     (local_state, local_decay), (local_entering, leads) = lax.scan(
         advance, (empty_state, unit_decay), (accumulated_sums_list, block_state)
     )
-    incoming_decay, incoming = carried_in(
-        (local_decay, local_state), "ctx", join_states, (unit_decay, empty_state)
-    )
+    incoming = carried_in((local_decay, local_state), "ctx")
     entering = local_entering + leads[..., None, None] * incoming
     carried = (
         jnp.einsum(
@@ -119,11 +99,17 @@
     normed = ((grouped * factor).reshape(tok_rows, width) * norm_gain.astype(jnp.float32)).astype(
         jnp.bfloat16
     )
-    terms = jnp.dot(
-        normed,
-        lax.all_gather(out_weight, "ctx", axis=1, tiled=True),
+    lanes = lax.axis_size("group")
+    span = width // lanes
+    mine = lax.dynamic_slice_in_dim(out_weight, lax.axis_index("group") * span, span, 0)
+    whole = lax.all_gather(mine, ("group", "ctx"))
+    whole = whole.reshape(lanes, lax.axis_size("ctx"), span, out_weight.shape[1])
+    terms = jnp.einsum(
+        "tgr,gcrn->tcn",
+        normed.reshape(tok_rows, lanes, span),
+        whole,
         preferred_element_type=jnp.float32,
-    )
+    ).reshape(tok_rows, -1)
     summed = lax.psum_scatter(terms.astype(jnp.bfloat16), "head", scatter_dimension=0, tiled=True)
     return summed
 

time: 479 us -> 390 us (0.81)
  waiting for transfers between devices: 371 us -> 263 us
  local copies, waits for them, and re-layouts: 23.7 us -> 47.8 us
  other arithmetic: 28.6 us -> 21.6 us
  blocking collectives: 5.74 us -> 0 us
    all_gather x2 -> x1, waiting for transfers between devices: 326 us -> 24.2 us  [shards(): whole = lax.all_gather(mine, ('group', 'ctx'))]
    ppermute x0 -> x3, waiting for transfers between devices: none -> 194 us  [carried_in(): incoming = lax.ppermute(total, axis, hops).astype(jnp.float32)]
    reshape x0 -> x1, local copies, waits for them, and re-layouts: none -> 21.6 us  [shards(): whole.reshape(lanes, lax.axis_size('ctx'), span, out_weight.shape[1])]
    select_n x4 -> x0, other arithmetic: 8.9 us -> none  [lap(): return jax.tree.map(lambda a, b: jnp.where(reached, a, b), new, before)]
    all_gather x1 -> x0, blocking collectives: 5.74 us -> none  [carried_in(): lax.all_gather(part.astype(kind), axis)]
  transfers between devices with their start and end apart: 3 -> 5, of which waited for: 3 -> 5; matrix products, arithmetic and copies ran while one was open for 7% -> 17% of each run, Pallas kernels for 0% -> 0%
where the time goes in v1:
time: 390 us; the launch traced here: 386 us
  waiting for transfers between devices  263 us (67%)
  local copies, waits for them, and re-layouts  47.8 us (12%)
  matrix products  36 us (9%)
  other arithmetic  21.6 us (6%)
  between operations  13.7 us (4%)
  starting transfers between devices  4.09 us (1%)
    ppermute x3, waiting for transfers between devices, carried_in(): incoming = lax.ppermute(total, axis, hops).astype(jnp.float32)  194 us
    reduce_scatter x1, waiting for transfers between devices, shards(): lax.psum_scatter(terms.astype(jnp.bfloat16), 'head', scatter_dimension=0,...  44.4 us
    all_gather x1, waiting for transfers between devices, shards(): whole = lax.all_gather(mine, ('group', 'ctx'))  24.2 us
    reshape x1, local copies, waits for them, and re-layouts, shards(): whole.reshape(lanes, lax.axis_size('ctx'), span, out_weight.shape[1])  21.6 us
    dot_general x1, matrix products, shards(): jnp.einsum('tgr,gcrn->tcn', normed.reshape(tok_rows, lanes, span), whole,...  13.9 us
    reshape x2, local copies, waits for them, and re-layouts, shards(): inputs = head_input.reshape(blocks, STRETCH, groups, per_group, HEADP)  13.8 us
    dot_general x1, matrix products, shards(): jnp.einsum('kqgn,kgjpn->kqgjp', out_maps.astype(jnp.float32), entering, p...  9.71 us
    add x4, other arithmetic, advance(): total[..., None, None] * state + piece  8.08 us
  transfers between devices with their start and end apart: 5, of which 5 were waited for; matrix products, arithmetic and copies ran while one was open for 17% of the time, Pallas kernels for 0%

profile of v1, /device:TPU:27, one launch (start us, length us, event | category | flops | bytes accessed | tf_op | source)
XLA Modules:
  0.0 385.8 jit_solution(16557162756791343365)
XLA Ops:
  6.5 3.1 constant_dynamic-slice_fusion
  9.8 7.1 %reshape.77 = bf16[4,128,2,16,64]{4,3,2,1,0:T(8,128)(2,1)} reshape(bf16[512,2048]{1,0:T(8,128)(2,1)} %param.11) | data formatting | bytes 4194304 | tf_op jit(solution)/shard_map/reshape | solution.py:64
  16.8 6.7 %copy.18 = bf16[4,128,2,16,64]{1,4,3,2,0:T(8,128)(2,1)} copy(bf16[4,128,2,16,64]{4,3,2,1,0:T(8,128)(2,1)} %reshape.77) | data formatting | bytes 4194304 | tf_op jit(solution)/shard_map/reshape | solution.py:64
  25.3 6.1 %fusion.22 = f32[4,2,16,64,256]{4,3,2,1,0:T(8,128)} fusion(bf16[4,128,2,16,64]{1,4,3,2,0:T(8,128)(2,1)} %copy.18, f32[4,128,2,16]{1,3,2,0:T(8,128)S(1)} %bitcast.91, bf16[4,128,2,256,1]{3,2,1,0,4:T(2,128)(2,1)S(1)} %bitcast.87), kind=kOutput, calls=%fused_computation.36 | convolution fusion | flops 540016640 | bytes 11075584 | tf_op jit(solution)/shard_map/ksgjp,ksgn->kgjpn/dot_general | solution.py:38
  31.3 14.3 %while.17 = (s32[]{:T(128)}, f32[2,16,64,256]{3,2,1,0:T(8,128)S(1)}, f32[2,16]{1,0:T(2,128)S(1)}, f32[4,2,16,64,256]{4,3,2,1,0:T(8,128)}, f32[4,2,16]{2,1,0:T(2,...) while((s32[]{:T(128)}, ...), condition=%wide.region_2.3_spmd.clone, body=%wide.region_1.2_spmd.clone.sunk | while | flops 2097251 | bytes 10489078 | solution.py:80
  31.4 1.5 bitcast_dynamic-update-slice_fusion.4
  32.9 2.0 bitcast_add_fusion.2
  35.0 1.5 bitcast_dynamic-update-slice_fusion.4
  36.5 2.0 bitcast_add_fusion.2
  38.5 1.5 bitcast_dynamic-update-slice_fusion.4
  40.1 2.0 bitcast_add_fusion.2
  43.6 2.0 bitcast_add_fusion.2
  47.2 65.5 %collective-permute-done = bf16[2,16,64,256]{3,2,1,0:T(8,128)(2,1)S(1)} collective-permute-done((bf16[2,16,64,256]{3,2,1,0:T(8,128)(2,1)S(1)}, bf16[2,16,64,256]{3,2,1,0:T(8,128)(2,1)S(1)}, u32[]{:S(2)}, u32[]{:S(2)}) %collective-permute-start) | collective-permute-done | bytes 1048608 | tf_op jit(solution)/shard_map/ppermute | solution.py:18
  116.5 4.0 %copy.23 = bf16[512,2048]{0,1:T(8,128)(2,1)} copy(bf16[512,2048]{1,0:T(8,128)(2,1)} %param.12) | data formatting | bytes 4194304 | tf_op args[1]
  120.5 63.5 %collective-permute-done.1 = bf16[2,16,64,256]{3,2,1,0:T(8,128)(2,1)} collective-permute-done((bf16[2,16,64,256]{3,2,1,0:T(8,128)(2,1)}, bf16[2,16,64,256]{3,2,1,0:T(8,128)(2,1)}, u32[]{:S(2)}, u32[]{:S(2)}) %collective-permute-start.1) | collective-permute-done | bytes 1048608 | tf_op jit(solution)/shard_map/ppermute | solution.py:18
  184.1 1.5 add_convert_fusion
  187.4 6.0 %fusion.4 = f32[4,2,16,128,64]{3,4,2,1,0:T(8,128)} fusion(bf16[4,128,2,16,64]{1,4,3,2,0:T(8,128)(2,1)S(1)} %copy-done.2, f32[4,2,16,128]{3,2,1,0:T(8,128)S(1)} %bitcast.92, f32[4,2,128,128]{3,2,1,0:T(8,128)S(1)} %fusion.29, f32[4,2,16,128]{3,2,1,0:T(8,128)S(1)} %bitcast.90, pred[128,128]{1,0:T(8,128)(4,1)S(1)} %iota_compare_fusion), kind=kOutput, calls=%fused_computation.15 | convolution fusion | flops 281018368 | bytes 6963200 | tf_op jit(solution)/shard_map/kgjqs,ksgjp->kqgjp/dot_general | solution.py:34
  193.4 64.9 %collective-permute-done.2 = bf16[2,16,64,256]{3,2,1,0:T(8,128)(2,1)S(1)} collective-permute-done((bf16[2,16,64,256]{3,2,1,0:T(8,128)(2,1)S(1)}, bf16[2,16,64,256]{3,2,1,0:T(8,128)(2,1)S(1)}, u32[]{:S(2)}, u32[]{:S(2)}) %collective-permute-start.2) | collective-permute-done | bytes 1048608 | tf_op jit(solution)/shard_map/ppermute | solution.py:18
  258.5 9.7 %fusion.6 = f32[4,128,2,16,64]{1,4,3,2,0:T(8,128)S(1)} fusion(bf16[4,128,2,16,64]{1,4,3,2,0:T(8,128)(2,1)S(1)} %copy-done.2, f32[4,2,16,128,64]{3,4,2,1,0:T(8,128)} %fusion.4, f32[2,16]{1,0:T(2,128)S(1)} %mul.149, f32[4,128,2,16]{1,3,2,0:T(8,128)S(1)} %exponential_bitcast_fusion, f32[4,2,16,64,256]{4,3,2,1,0:T(8,128)} %get-tuple-element.45, ...), kind=kOutput, calls=%fused_computation.17 | convolution fusion | flops 3230662656 | bytes 21561984 | tf_op jit(solution)/shard_map/kqgn,kgjpn->kqgjp/dot_general | solution.py:86
  268.3 3.6 copy.22
  274.8 24.2 %all-gather.3.cloned.1.call-done = bf16[8192,1024]{1,0:T(8,128)(2,1)} async-done(((bf16[1024,1024]{1,0:T(8,128)(2,1)}), bf16[8192,1024]{1,0:T(8,128)(2,1)}) %all-gather.3.cloned.1.call-update) | async-done | bytes 16777232 | tf_op jit(solution)/shard_map/all_gather | solution.py:105
  299.0 21.6 %copy.24 = bf16[2,4,1024,1024]{2,3,1,0:T(8,128)(2,1)} copy(bf16[2,4,1024,1024]{3,2,1,0:T(8,128)(2,1)} %bitcast.85) | data formatting | bytes 33554432 | tf_op jit(solution)/shard_map/reshape | solution.py:106
  320.6 13.9 %bitcast_convert_fusion = bf16[512,4096]{1,0:T(8,128)(2,1)} fusion(bf16[512,2,1024]{0,2,1:T(8,128)(2,1)S(1)} %bitcast.88, bf16[4096,2,1024]{2,0,1:T(8,128)(2,1)} %bitcast.86), kind=kOutput, calls=%fused_computation.6 | convolution fusion | flops 8592031744 | bytes 23068672 | tf_op jit(solution)/shard_map/tgr,gcrn->tcn/dot_general | solution.py:107
  334.5 44.4 %reduce-scatter.2.cloned.1.call-done = bf16[128,4096]{1,0:T(8,128)(2,1)} async-done(((bf16[512,4096]{1,0:T(8,128)(2,1)}), bf16[128,4096]{1,0:T(8,128)(2,1)}) %reduce-scatter.2.cloned.1.call-update) | async-done | bytes 1048592 | tf_op jit(solution)/shard_map/reduce_scatter | solution.py:113
  (56 shorter events, 13.6 us)
Async XLA Ops:
  6.5 18.6 %copy-start = (f32[32,512]{1,0:T(8,128)S(1)}, f32[32,512]{1,0:T(8,128)}, u32[]{:S(2)}) copy-start(f32[32,512]{1,0:T(8,128)} %param.15) | copy-start | bytes 196612
  6.5 292.4 %all-gather.3.cloned.1.call-start = ((), (), s32[]{:S(2)}) async-start(), calls=%async_computation.2 | async-start | bytes 18874368 | tf_op jit(solution)/shard_map/all_gather | solution.py:105
  9.7 369.2 %reduce-scatter.2.cloned.1.call-start = ((), (), s32[]{:S(2)}) async-start(), calls=%async_computation.1 | async-start | bytes 5242880 | tf_op jit(solution)/shard_map/reduce_scatter | solution.py:113
  16.8 6.7 %copy-start.4 = (bf16[512,512]{1,0:T(8,128)(2,1)S(1)}, bf16[512,512]{1,0:T(8,128)(2,1)}, u32[]{:S(2)}) copy-start(bf16[512,512]{1,0:T(8,128)(2,1)} %param.13) | copy-start | bytes 1572868
  16.8 6.8 %copy-start.5 = (f32[32,512]{1,0:T(8,128)S(1)}, f32[32,512]{1,0:T(8,128)}, u32[]{:S(2)}) copy-start(f32[32,512]{1,0:T(8,128)} %param.16) | copy-start | bytes 196612
  45.7 70.7 %copy-start.7 = (f32[32]{0:T(128)S(1)}, f32[32]{0:T(128)}, u32[]{:S(2)}) copy-start(f32[32]{0:T(128)} %param.17) | copy-start | bytes 388
  45.9 74.6 %copy-start.6 = (bf16[2048]{0:T(1024)(128)(2,1)S(1)}, bf16[2048]{0:T(1024)(128)(2,1)}, u32[]{:S(2)}) copy-start(bf16[2048]{0:T(1024)(128)(2,1)} %param.18) | copy-start | bytes 12292
  45.9 66.8 %collective-permute-start = (bf16[2,16,64,256]{3,2,1,0:T(8,128)(2,1)S(1)}, bf16[2,16,64,256]{3,2,1,0:T(8,128)(2,1)S(1)}, u32[]{:S(2)}, u32[]{:S(2)}) collective-permute-start(bf16[2,16,64,256]{3,2,1,0:T(8,128)(2,1)S(1)} %add_convert_fusion.2), channel_id=1, source_target_pairs={{0,4},{4,8},{8,12},{1,5},{5,9},{9,13},{2,6},{6,10},{10,14},{3,7},{... | collective-permute-start | bytes 3145736 | tf_op jit(solution)/shard_map/ppermute | solution.py:18
  114.0 70.1 %collective-permute-start.1 = (bf16[2,16,64,256]{3,2,1,0:T(8,128)(2,1)}, bf16[2,16,64,256]{3,2,1,0:T(8,128)(2,1)}, u32[]{:S(2)}, u32[]{:S(2)}) collective-permute-start(bf16[2,16,64,256]{3,2,1,0:T(8,128)(2,1)} %add_convert_fusion.1), channel_id=1, source_target_pairs={{0,4},{4,8},{8,12},{1,5},{5,9},{9,13},{2,6},{6,10},{10,14},{3,7},{... | collective-permute-start | bytes 3145736 | tf_op jit(solution)/shard_map/ppermute | solution.py:18
  120.5 66.9 %copy-start.2 = (bf16[4,128,2,16,64]{1,4,3,2,0:T(8,128)(2,1)S(1)}, bf16[4,128,2,16,64]{1,4,3,2,0:T(8,128)(2,1)}, u32[]{:S(2)}) copy-start(bf16[4,128,2,16,64]{1,4,3,2,0:T(8,128)(2,1)} %copy.18) | copy-start | bytes 6291460
  185.6 72.7 %collective-permute-start.2 = (bf16[2,16,64,256]{3,2,1,0:T(8,128)(2,1)S(1)}, bf16[2,16,64,256]{3,2,1,0:T(8,128)(2,1)S(1)}, u32[]{:S(2)}, u32[]{:S(2)}) collective-permute-start(bf16[2,16,64,256]{3,2,1,0:T(8,128)(2,1)S(1)} %add_convert_fusion), channel_id=1, source_target_pairs={{0,4},{4,8},{8,12},{1,5},{5,9},{9,13},{2,6},{6,10},{10,14},{3,7},{... | collective-permute-start | bytes 3145736 | tf_op jit(solution)/shard_map/ppermute | solution.py:18
  268.3 3.6 copy-start.3
  320.6 58.4 %copy-start.1 = (f32[32,512]{1,0:T(8,128)S(1)}, f32[32,512]{1,0:T(8,128)}, u32[]{:S(2)}) copy-start(f32[32,512]{1,0:T(8,128)} %param.15) | copy-start | bytes 196612
Sparse Core Ops, SparseCore 0:
  9.8 289.1 all-gather.2
  334.6 44.2 reduce-scatter.1

commit v2 on v1

v2 whole, which is shorter than its diff:
```python
import functools

import jax
import jax.numpy as jnp
from jax import lax
from jax.experimental import pallas as pl
from jax.experimental.pallas import tpu as pltpu
from jax.sharding import PartitionSpec as P

HEADP = 64
STATE = 256
STRETCH = 128
PIECES = 2
QUARTERS = 4
MESH = pl.DeviceIdType.MESH
F32 = jnp.float32
BF16 = jnp.bfloat16


def rows_of(k, size):
    return pl.ds(pl.multiple_of(k * size, size), size)


def layer(
    sizes,
    x_ref,
    gate_ref,
    bm_ref,
    cm_ref,
    step_ref,
    dec_ref,
    skip_ref,
    gain_ref,
    w_ref,
    out_ref,
    wg,
    part,
    rs,
    y_ref,
    st,
    ent,
    inc,
    sbuf,
    normed,
    expander,
    ramp_t,
    rows_r,
    lead_ref,
    full_ref,
    local_sem,
    w_recv,
    up_send,
    down_send,
    side_send,
    st_send,
    st_recv,
    rs_send,
    rs_recv,
):
    lanes, ctx, peers = sizes
    tokens, width = x_ref.shape
    heads = step_ref.shape[0]
    groups = bm_ref.shape[1] // STATE
    blocks = tokens // STRETCH
    chunks, depth, cw = wg.shape[1:]
    share = lanes == 2 and chunks % 2 == 0
    line_chunks = chunks // 2 if share else chunks
    units = (ctx - 1) * line_chunks
    slots = units * PIECES
    span = depth // PIECES
    gw = width // groups
    qw = width // QUARTERS
    owned = tokens // peers
    y, z, me = lax.axis_index("group"), lax.axis_index("ctx"), lax.axis_index("head")
    above, below = z + 1 < ctx, z > 0
    other = {"group": 1 - y} if share else None

    barrier = pltpu.get_barrier_semaphore()

    @pl.when(above)
    def _():
        pl.semaphore_signal(barrier, inc=1, device_id={"ctx": z + 1}, device_id_type=MESH)

    @pl.when(below)
    def _():
        pl.semaphore_signal(barrier, inc=1, device_id={"ctx": z - 1}, device_id_type=MESH)

    if share:
        pl.semaphore_signal(barrier, inc=1, device_id=other, device_id_type=MESH)
    for d in range(1, peers):
        pl.semaphore_signal(
            barrier, inc=1, device_id={"head": lax.rem(me + d, peers)}, device_id_type=MESH
        )
    ends = jnp.where(above, 1, 0) + jnp.where(below, 1, 0)
    pl.semaphore_wait(barrier, peers - 1 + (1 if share else 0) + ends)

    def line_chunk(i):
        return 2 * i + y if share else i

    def piece(j, c, r):
        return wg.at[j, c, rows_of(r, span)]

    def send(src, j, c, r, sem, target):
        return pltpu.make_async_remote_copy(
            src_ref=src,
            dst_ref=piece(j, c, r),
            send_sem=sem.at[j, c, r],
            recv_sem=w_recv.at[j, c, r],
            device_id=target,
            device_id_type=MESH,
        )

    def own_piece(c, r):
        return w_ref.at[rows_of(r, span), rows_of(c, cw)]

    def arrived(j, c, r):
        send(piece(j, c, r), j, c, r, up_send, {"head": lax.rem(me + 1, peers)}).wait_recv()

    def own_sends(i, wait):
        c, r = line_chunk(lax.div(i, PIECES)), lax.rem(i, PIECES)
        for flag, sem, target in ((above, up_send, z + 1), (below, down_send, z - 1)):

            @pl.when(flag)
            def _():
                copy = send(own_piece(c, r), z, c, r, sem, {"ctx": target})
                if wait:
                    copy.wait_send()
                else:
                    copy.start()

    def each(count, body):
        def go(i, carry):
            body(i)
            return carry

        lax.fori_loop(0, count, go, 0)

    each(line_chunks * PIECES, lambda i: own_sends(i, False))

    def local_copy(c):
        return pltpu.make_async_copy(w_ref.at[:, rows_of(c, cw)], wg.at[z, c], local_sem.at[c])

    each(chunks, lambda c: local_copy(c).start())

    def service(slot, wait=False):
        unit, r = lax.div(slot, PIECES), lax.rem(slot, PIECES)
        s, c = lax.div(unit, line_chunks), line_chunk(lax.rem(unit, line_chunks))
        for j, valid, more, sem, target in (
            (z - 1 - s, z - 1 - s >= 0, above, up_send, z + 1),
            (z + 1 + s, z + 1 + s < ctx, below, down_send, z - 1),
        ):

            @pl.when(jnp.logical_and(valid, slot < slots))
            def _():
                if not wait:
                    arrived(j, c, r)

                @pl.when(more)
                def _():
                    copy = send(piece(j, c, r), j, c, r, sem, {"ctx": target})
                    if wait:
                        copy.wait_send()
                    else:
                        copy.start()

                if share:
                    copy = send(piece(j, c, r), j, c, r, side_send, other)
                    if wait:
                        copy.wait_send()
                    else:
                        copy.start()

    spots = lax.broadcasted_iota(jnp.int32, (heads, width), 1)
    owner = lax.broadcasted_iota(jnp.int32, (heads, width), 0)
    inside = jnp.logical_and(spots >= owner * HEADP, spots < owner * HEADP + HEADP)
    expander[...] = jnp.where(inside, 1.0, 0.0).astype(BF16)

    def spread(v, lo, size):
        high = v.astype(BF16)
        low = (v - high.astype(F32)).astype(BF16)
        e = expander[:, lo : lo + size]
        return jnp.dot(high, e, preferred_element_type=F32) + jnp.dot(
            low, e, preferred_element_type=F32
        )

    row_i = lax.broadcasted_iota(jnp.int32, (STRETCH, STRETCH), 0)
    col_i = lax.broadcasted_iota(jnp.int32, (STRETCH, STRETCH), 1)
    lower = row_i >= col_i
    nt = (((1,), (1,)), ((), ()))
    tn = (((0,), (0,)), ((), ()))

    st[...] = jnp.zeros_like(st)

    def states(k, lead):
        rows = rows_of(k, STRETCH)
        low_tri = jnp.where(lower, 1.0, 0.0).astype(F32)
        eye = jnp.where(row_i == col_i, 1.0, 0.0).astype(F32)
        logd = jnp.log(dec_ref[:, rows])
        logs = jnp.log(step_ref[:, rows])
        exact = functools.partial(
            lax.dot_general,
            dimension_numbers=nt,
            precision=lax.Precision.HIGHEST,
            preferred_element_type=F32,
        )
        ramp = exact(logd, low_tri)
        rt = exact(low_tri, logd)
        st_t = exact(eye, logs)
        rows_r[k] = ramp - logs
        ramp_t[k] = rt
        lead_ref[k] = lead
        end = rt[STRETCH - 1 : STRETCH, :]
        tails = jnp.exp(end - (rt - st_t))
        total = jnp.broadcast_to(jnp.exp(end), (8, heads))
        for g in range(groups):
            cols = slice(g * gw, (g + 1) * gw)
            weighted = (x_ref[rows, cols].astype(F32) * spread(tails, g * gw, gw)).astype(BF16)
            made = lax.dot_general(
                bm_ref[rows, g * STATE : (g + 1) * STATE],
                weighted,
                tn,
                preferred_element_type=F32,
            )
            old = st[:, cols]
            ent[k, :, cols] = old.astype(BF16)
            st[:, cols] = spread(total, g * gw, gw)[0:1] * old + made
        return lead + jnp.broadcast_to(end, (8, heads))

    lead = lax.fori_loop(0, blocks, states, jnp.zeros((8, heads), F32))
    full_ref[...] = jnp.exp(lead)

    def state_copy(q):
        return pltpu.make_async_remote_copy(
            src_ref=sbuf.at[q],
            dst_ref=inc.at[q],
            send_sem=st_send.at[q],
            recv_sem=st_recv.at[q],
            device_id={"ctx": z + 1},
            device_id_type=MESH,
        )

    @pl.when(z == 0)
    def _():
        for q in range(QUARTERS):
            inc[q] = jnp.zeros_like(inc[q])
            sbuf[q] = st[:, q * qw : (q + 1) * qw].astype(BF16)

            @pl.when(above)
            def _():
                state_copy(q).start()

    service(0)

    def chain():
        for q in range(QUARTERS):
            pltpu.make_async_remote_copy(
                src_ref=sbuf.at[q],
                dst_ref=inc.at[q],
                send_sem=st_send.at[q],
                recv_sem=st_recv.at[q],
                device_id={"ctx": z - 1},
                device_id_type=MESH,
            ).wait_recv()

            @pl.when(above)
            def _():
                fall = spread(full_ref[...], q * qw, qw)[0:1]
                held = st[:, q * qw : (q + 1) * qw]
                sbuf[q] = (fall * inc[q].astype(F32) + held).astype(BF16)
                state_copy(q).start()

    half = lax.broadcasted_iota(jnp.int32, (STRETCH, 2 * HEADP), 1) < HEADP
    keep_lo = jnp.where(half, 1.0, 0.0).astype(BF16)
    keep_hi = jnp.where(half, 0.0, 1.0).astype(BF16)
    per_group = heads // groups

    def own_block(k, carry):
        rows = rows_of(k, STRETCH)
        rt = ramp_t[k]
        rr = rows_r[k]
        entry = jnp.exp(rt)
        for g in range(groups):
            c_map = cm_ref[rows, g * STATE : (g + 1) * STATE]
            b_map = bm_ref[rows, g * STATE : (g + 1) * STATE]
            scores = lax.dot_general(c_map, b_map, nt, preferred_element_type=F32)
            cols = slice(g * gw, (g + 1) * gw)
            skip = spread(jnp.broadcast_to(skip_ref[...], (8, heads)), g * gw, gw)[0:1]
            y_ref[rows, cols] = (
                jnp.dot(c_map, ent[k, :, cols], preferred_element_type=F32)
                * spread(entry, g * gw, gw)
                + skip * x_ref[rows, cols].astype(F32)
            )
            for pair in range(per_group // 2):
                mixes = []
                for h in (g * per_group + 2 * pair, g * per_group + 2 * pair + 1):
                    fade = jnp.where(lower, rt[:, h : h + 1] - rr[h : h + 1, :], -1e30)
                    mixes.append((scores * jnp.exp(fade)).astype(BF16))
                at = slice(g * gw + pair * 2 * HEADP, g * gw + (pair + 1) * 2 * HEADP)
                both = x_ref[rows, at]
                y_ref[rows, at] += jnp.dot(
                    jnp.concatenate(mixes, axis=1),
                    jnp.concatenate([both * keep_lo, both * keep_hi], axis=0),
                    preferred_element_type=F32,
                )

        @pl.when(jnp.logical_and(below, jnp.minimum(z - 1, blocks - 1) == k))
        def _():
            chain()

        service(1 + k)
        return carry

    lax.fori_loop(0, blocks, own_block, 0)

    def finish_block(k, carry):
        rows = rows_of(k, STRETCH)
        reach = jnp.exp(ramp_t[k] + lead_ref[k, 0:1])
        squares = [jnp.zeros((STRETCH, 1), F32) for _ in range(groups)]
        for q in range(QUARTERS):
            g = q * qw // gw
            cols = slice(q * qw, (q + 1) * qw)
            carried = jnp.dot(
                cm_ref[rows, g * STATE : (g + 1) * STATE], inc[q], preferred_element_type=F32
            )
            gate = gate_ref[rows, cols].astype(F32)
            gated = (y_ref[rows, cols] + carried * spread(reach, q * qw, qw)) * (
                gate / (1.0 + jnp.exp(-gate))
            )
            y_ref[rows, cols] = gated
            squares[g] = squares[g] + jnp.sum(gated * gated, axis=1, keepdims=True)
        for g in range(groups):
            cols = slice(g * gw, (g + 1) * gw)
            factor = lax.rsqrt(squares[g] / gw + 1e-05)
            normed[rows, cols] = (y_ref[rows, cols] * factor * gain_ref[:, cols].astype(F32)).astype(
                BF16
            )

        @pl.when(lax.rem(k, 2) == 1)
        def _():
            service(1 + blocks + lax.div(k, 2))

        return carry

    lax.fori_loop(0, blocks, finish_block, 0)
    first = 1 + blocks + blocks // 2

    def partial_copy(d, j, c):
        peer = lax.rem(me + d, peers)
        return pltpu.make_async_remote_copy(
            src_ref=part.at[j, c, rows_of(peer, owned)],
            dst_ref=rs.at[d - 1, j, c],
            send_sem=rs_send.at[d - 1, j, c],
            recv_sem=rs_recv.at[d - 1, j, c],
            device_id={"head": peer},
            device_id_type=MESH,
        )

    entries = max(chunks, 4 if share else 2)

    def locate(v, e):
        own = v == 0
        line = e < 2
        unit = jnp.where(line, v - 1, v - 2)
        known = jnp.logical_and(unit >= 0, unit < units)
        safe = jnp.where(known, unit, 0)
        s, i = lax.div(safe, line_chunks), lax.rem(safe, line_chunks)
        j = jnp.where(lax.rem(e, 2) == 0, z - 1 - s, z + 1 + s)
        if share:
            c = jnp.where(line, 2 * i + y, 2 * i + 1 - y)
        else:
            c = i
        known = jnp.logical_and(known, e < (4 if share else 2))
        known = jnp.logical_and(known, jnp.logical_and(j >= 0, j < ctx))
        valid = jnp.where(own, e < chunks, known)
        return own, line, jnp.where(own, z, j), jnp.where(own, e, c), valid

    def project(v, e):
        own, line, j, c, valid = locate(v, e)

        @pl.when(jnp.logical_and(valid, own))
        def _():
            local_copy(c).wait()

        @pl.when(jnp.logical_and(valid, jnp.logical_not(jnp.logical_or(own, line))))
        def _():
            for r in range(PIECES):
                arrived(j, c, r)

        @pl.when(valid)
        def _():
            part[j, c] = jnp.dot(normed[...], wg[j, c], preferred_element_type=F32).astype(BF16)
            for d in range(1, peers):
                partial_copy(d, j, c).start()

    def collect(v, e):
        own, line, j, c, valid = locate(v, e)

        @pl.when(valid)
        def _():
            total = part[j, c, rows_of(me, owned)].astype(F32)
            for d in range(1, peers):
                partial_copy(d, j, c).wait_recv()
                total = total + rs[d - 1, j, c].astype(F32)
            out_ref[:, rows_of(j * chunks + c, cw)] = total.astype(BF16)

    def rounds(v):
        @pl.when(jnp.logical_and(v >= 1, v <= units))
        def _():
            for r in range(PIECES):
                slot = (v - 1) * PIECES + r

                @pl.when(slot >= first)
                def _():
                    service(slot)

        each(entries, lambda e: project(v, e))

    each(units + 2, rounds)
    each(units + 2, lambda v: each(entries, lambda e: collect(v, e)))

    each(line_chunks * PIECES, lambda i: own_sends(i, True))
    each(slots, lambda i: service(i, True))

    @pl.when(above)
    def _():
        for q in range(QUARTERS):
            state_copy(q).wait_send()

    def sent(u):
        j, c = lax.div(u, chunks), lax.rem(u, chunks)
        for d in range(1, peers):
            partial_copy(d, j, c).wait_send()

    each(ctx * chunks, sent)


def shards(
    sizes,
    head_input,
    gate_input,
    input_map,
    output_map,
    step_size,
    decays,
    bypass_scale,
    norm_gain,
    out_weight,
):
    lanes, ctx, peers = sizes
    tokens, width = head_input.shape
    heads = step_size.shape[0]
    blocks = tokens // STRETCH
    depth, cols = out_weight.shape
    cw = min(cols, 256)
    chunks = cols // cw
    owned = tokens // peers
    dma = pltpu.SemaphoreType.DMA
    vmem = pl.BlockSpec(memory_space=pltpu.VMEM)
    return pl.pallas_call(
        functools.partial(layer, sizes),
        out_shape=jax.ShapeDtypeStruct((owned, ctx * cols), BF16),
        in_specs=[vmem] * 8 + [pl.BlockSpec(memory_space=pl.ANY)],
        out_specs=vmem,
        scratch_shapes=[
            pltpu.VMEM((ctx, chunks, depth, cw), BF16),
            pltpu.VMEM((ctx, chunks, tokens, cw), BF16),
            pltpu.VMEM((peers - 1, ctx, chunks, owned, cw), BF16),
            pltpu.VMEM((tokens, width), F32),
            pltpu.VMEM((STATE, width), F32),
            pltpu.VMEM((blocks, STATE, width), BF16),
            pltpu.VMEM((QUARTERS, STATE, width // QUARTERS), BF16),
            pltpu.VMEM((QUARTERS, STATE, width // QUARTERS), BF16),
            pltpu.VMEM((tokens, width), BF16),
            pltpu.VMEM((heads, width), BF16),
            pltpu.VMEM((blocks, STRETCH, heads), F32),
            pltpu.VMEM((blocks, heads, STRETCH), F32),
            pltpu.VMEM((blocks, 8, heads), F32),
            pltpu.VMEM((8, heads), F32),
            dma((chunks,)),
            dma((ctx, chunks, PIECES)),
            dma((ctx, chunks, PIECES)),
            dma((ctx, chunks, PIECES)),
            dma((ctx, chunks, PIECES)),
            dma((QUARTERS,)),
            dma((QUARTERS,)),
            dma((peers - 1, ctx, chunks)),
            dma((peers - 1, ctx, chunks)),
        ],
        compiler_params=pltpu.CompilerParams(
            collective_id=0, has_side_effects=True, vmem_limit_bytes=60 << 20
        ),
    )(
        head_input,
        gate_input,
        input_map,
        output_map,
        step_size,
        decays,
        bypass_scale.reshape(1, heads),
        norm_gain.reshape(1, width),
        out_weight,
    )


def solution(mesh):
    sizes = (mesh.shape["group"], mesh.shape["ctx"], mesh.shape["head"])
    return jax.shard_map(
        functools.partial(shards, sizes),
        mesh=mesh,
        in_specs=(
            P(("group", "ctx"), "head"),
            P(("group", "ctx"), "head"),
            P(("group", "ctx"), "head"),
            P(("group", "ctx"), "head"),
            P("head", ("group", "ctx")),
            P("head", ("group", "ctx")),
            P("head"),
            P("head"),
            P("head", "ctx"),
        ),
        out_specs=P(("group", "ctx", "head"), None),
        check_vma=False,
    )
```

time: 390 us -> 210 us (0.54); the launches traced: 386 us -> 210 us
  waiting for transfers between devices: 263 us -> 0 us
  Pallas kernels: 0 us -> 206 us
  local copies, waits for them, and re-layouts: 47.8 us -> 3.58 us
  matrix products: 36 us -> 0 us
  other arithmetic: 21.6 us -> 0 us
  between operations: 13.7 us -> 0.01 us
  starting transfers between devices: 4.09 us -> 0 us
    pallas_call x0 -> x1, Pallas kernels: none -> 206 us  [shards(): pl.pallas_call(functools.partial(layer, sizes), out_shape=jax.ShapeDtypeS...]
    ppermute x3 -> x0, waiting for transfers between devices: 194 us -> none  [carried_in(): incoming = lax.ppermute(total, axis, hops).astype(jnp.float32)]
    reduce_scatter x1 -> x0, waiting for transfers between devices: 44.4 us -> none  [shards(): lax.psum_scatter(terms.astype(jnp.bfloat16), 'head', scatter_dimension=0,...]
    dot_general x5 -> x0, matrix products: 36 us -> none  [the longest x1 13.9 us: shards(): jnp.einsum('tgr,gcrn->tcn', normed.reshape(tok_rows, lanes, span), whole,...]
    reshape x6 -> x1, local copies, waits for them, and re-layouts: 36.7 us -> 1.29 us  [shards(): norm_gain.reshape(1, width)]
    all_gather x1 -> x0, waiting for transfers between devices: 24.2 us -> none  [shards(): whole = lax.all_gather(mine, ('group', 'ctx'))]
    add x4 -> x0, other arithmetic: 8.08 us -> none  [advance(): total[..., None, None] * state + piece]
    dynamic_update_slice x8 -> x0, other arithmetic: 6.08 us -> none  [shards(): lax.scan(advance, (empty_state, unit_decay), (accumulated_sums_list, bloc...]
  transfers between devices with their start and end apart: 5 -> 0, of which waited for: 5 -> 0; matrix products, arithmetic and copies ran while one was open for 17% -> 0% of each run, Pallas kernels for 0% -> 0%
where the time goes in v2:
time: 210 us
  Pallas kernels  206 us (98%)
  local copies, waits for them, and re-layouts  3.58 us (2%)
    pallas_call x1, Pallas kernels, shards(): pl.pallas_call(functools.partial(layer, sizes), out_shape=jax.ShapeDtypeS...  206 us

profile of v2, /device:TPU:27, one launch (start us, length us, event | category | flops | bytes accessed | tf_op | source)
XLA Modules:
  0.0 209.9 jit_solution(15065627446104417151)
XLA Ops:
  0.0 1.3 reshape.7.gain_ref
  1.3 206.4 %shard_map.91 = bf16[128,4096]{1,0:T(8,128)(2,1)} custom-call(bf16[512,2048]{1,0:T(8,128)(2,1)} %x_ref.1, bf16[512,2048]{1,0:T(8,128)(2,1)} %gate_ref.1, bf16[512,512]{1,0:T(8,128)(2,1)} %bm_ref.1, bf16[512,512]{1,0:T(8,128)(2,1)} %cm_ref.1, f32[32,512]{1,0:T(8,128)} %step_ref.1, f32[32,512]{1,0:T(8,128)} %dec_ref.1, f32[1,32]{1,0:T(1,128)} %bitcast.1, ...), custom_call_target="tpu_custom_call" | custom-call | tf_op jit(solution)/shard_map/pallas_call | solution.py:459
  207.7 2.3 %copy.11 = bf16[128,4096]{1,0:T(8,128)(2,1)} copy(bf16[128,4096]{1,0:T(8,128)(2,1)} %shard_map.91) | data formatting | bytes 2097152

commit v3 on v2

--- a/solution.py
+++ b/solution.py
@@ -10,7 +10,8 @@
 HEADP = 64
 STATE = 256
 STRETCH = 128
-PIECES = 2
+PIECES = 4
+DELAY = 2
 QUARTERS = 4
 MESH = pl.DeviceIdType.MESH
 F32 = jnp.float32
@@ -116,17 +117,26 @@
     def arrived(j, c, r):
         send(piece(j, c, r), j, c, r, up_send, {"head": lax.rem(me + 1, peers)}).wait_recv()
 
-    def own_sends(i, wait):
+    own_count = line_chunks * PIECES
+    early = jnp.where(z == ctx - 2, own_count // 2, 0)
+
+    def own_send(i, flag, sem, target, wait=False):
         c, r = line_chunk(lax.div(i, PIECES)), lax.rem(i, PIECES)
-        for flag, sem, target in ((above, up_send, z + 1), (below, down_send, z - 1)):
-
-            @pl.when(flag)
-            def _():
-                copy = send(own_piece(c, r), z, c, r, sem, {"ctx": target})
-                if wait:
-                    copy.wait_send()
-                else:
-                    copy.start()
+
+        @pl.when(flag)
+        def _():
+            copy = send(own_piece(c, r), z, c, r, sem, {"ctx": target})
+            if wait:
+                copy.wait_send()
+            else:
+                copy.start()
+
+    def own_down(i, wait=False):
+        own_send(i, below, down_send, z - 1, wait)
+
+    def own_up(i, first_part):
+        now = (i < early) if first_part else (i >= early)
+        own_send(i, jnp.logical_and(above, now), up_send, z + 1)
 
     def each(count, body):
         def go(i, carry):
@@ -135,22 +145,30 @@
 
         lax.fori_loop(0, count, go, 0)
 
-    each(line_chunks * PIECES, lambda i: own_sends(i, False))
+    each(own_count, own_down)
+    each(own_count, lambda i: own_up(i, True))
 
     def local_copy(c):
         return pltpu.make_async_copy(w_ref.at[:, rows_of(c, cw)], wg.at[z, c], local_sem.at[c])
 
     each(chunks, lambda c: local_copy(c).start())
 
-    def service(slot, wait=False):
-        unit, r = lax.div(slot, PIECES), lax.rem(slot, PIECES)
-        s, c = lax.div(unit, line_chunks), line_chunk(lax.rem(unit, line_chunks))
-        for j, valid, more, sem, target in (
-            (z - 1 - s, z - 1 - s >= 0, above, up_send, z + 1),
-            (z + 1 + s, z + 1 + s < ctx, below, down_send, z - 1),
-        ):
-
-            @pl.when(jnp.logical_and(valid, slot < slots))
+    late = jnp.where(z == ctx - 1, 0, DELAY)
+
+    def service(at, wait=False):
+        for up in (True, False):
+            slot = at - late * PIECES if up and not wait else at
+            fits = jnp.logical_and(slot >= 0, slot < slots)
+            slot = jnp.where(fits, slot, 0)
+            unit, r = lax.div(slot, PIECES), lax.rem(slot, PIECES)
+            s, c = lax.div(unit, line_chunks), line_chunk(lax.rem(unit, line_chunks))
+            if up:
+                j, more, sem, target = z - 1 - s, above, up_send, z + 1
+            else:
+                j, more, sem, target = z + 1 + s, below, down_send, z - 1
+            valid = jnp.logical_and(j >= 0, j < ctx)
+
+            @pl.when(jnp.logical_and(valid, fits))
             def _():
                 if not wait:
                     arrived(j, c, r)
@@ -249,7 +267,7 @@
             def _():
                 state_copy(q).start()
 
-    service(0)
+        each(own_count, lambda i: own_up(i, False))
 
     def chain():
         for q in range(QUARTERS):
@@ -303,14 +321,16 @@
                     preferred_element_type=F32,
                 )
 
-        @pl.when(jnp.logical_and(below, jnp.minimum(z - 1, blocks - 1) == k))
-        def _():
-            chain()
-
-        service(1 + k)
         return carry
 
     lax.fori_loop(0, blocks, own_block, 0)
+    service(0)
+    service(1)
+
+    @pl.when(below)
+    def _():
+        chain()
+        each(own_count, lambda i: own_up(i, False))
 
     def finish_block(k, carry):
         rows = rows_of(k, STRETCH)
@@ -335,14 +355,11 @@
                 BF16
             )
 
-        @pl.when(lax.rem(k, 2) == 1)
-        def _():
-            service(1 + blocks + lax.div(k, 2))
-
+        service(2 + k)
         return carry
 
     lax.fori_loop(0, blocks, finish_block, 0)
-    first = 1 + blocks + blocks // 2
+    first = 2 + blocks
 
     def partial_copy(d, j, c):
         peer = lax.rem(me + d, peers)
@@ -360,11 +377,12 @@
     def locate(v, e):
         own = v == 0
         line = e < 2
-        unit = jnp.where(line, v - 1, v - 2)
+        rising = lax.rem(e, 2) == 0
+        unit = jnp.where(line, v - 1, v - 2) - jnp.where(rising, late, 0)
         known = jnp.logical_and(unit >= 0, unit < units)
         safe = jnp.where(known, unit, 0)
         s, i = lax.div(safe, line_chunks), lax.rem(safe, line_chunks)
-        j = jnp.where(lax.rem(e, 2) == 0, z - 1 - s, z + 1 + s)
+        j = jnp.where(rising, z - 1 - s, z + 1 + s)
         if share:
             c = jnp.where(line, 2 * i + y, 2 * i + 1 - y)
         else:
@@ -404,7 +422,7 @@
             out_ref[:, rows_of(j * chunks + c, cw)] = total.astype(BF16)
 
     def rounds(v):
-        @pl.when(jnp.logical_and(v >= 1, v <= units))
+        @pl.when(jnp.logical_and(v >= 1, v <= units + DELAY))
         def _():
             for r in range(PIECES):
                 slot = (v - 1) * PIECES + r
@@ -415,10 +433,11 @@
 
         each(entries, lambda e: project(v, e))
 
-    each(units + 2, rounds)
-    each(units + 2, lambda v: each(entries, lambda e: collect(v, e)))
-
-    each(line_chunks * PIECES, lambda i: own_sends(i, True))
+    each(units + 2 + DELAY, rounds)
+    each(units + 2 + DELAY, lambda v: each(entries, lambda e: collect(v, e)))
+
+    each(own_count, lambda i: own_down(i, True))
+    each(own_count, lambda i: own_send(i, above, up_send, z + 1, True))
     each(slots, lambda i: service(i, True))
 
     @pl.when(above)

time: 210 us -> 190 us (0.905)
  Pallas kernels: 206 us -> 187 us
    pallas_call x1, Pallas kernels: 206 us -> 187 us  [shards(): pl.pallas_call(functools.partial(layer, sizes), out_shape=jax.ShapeDtypeS...]
where the time goes in v3:
time: 190 us
  Pallas kernels  187 us (98%)
  local copies, waits for them, and re-layouts  3.58 us (2%)
    pallas_call x1, Pallas kernels, shards(): pl.pallas_call(functools.partial(layer, sizes), out_shape=jax.ShapeDtypeS...  187 us

profile of v3, /device:TPU:27, one launch (start us, length us, event | category | flops | bytes accessed | tf_op | source)
XLA Modules:
  0.0 190.3 jit_solution(7107168500877082638)
XLA Ops:
  0.0 1.3 reshape.7.gain_ref
  1.3 186.7 %shard_map.91 = bf16[128,4096]{1,0:T(8,128)(2,1)} custom-call(bf16[512,2048]{1,0:T(8,128)(2,1)} %x_ref.1, bf16[512,2048]{1,0:T(8,128)(2,1)} %gate_ref.1, bf16[512,512]{1,0:T(8,128)(2,1)} %bm_ref.1, bf16[512,512]{1,0:T(8,128)(2,1)} %cm_ref.1, f32[32,512]{1,0:T(8,128)} %step_ref.1, f32[32,512]{1,0:T(8,128)} %dec_ref.1, f32[1,32]{1,0:T(1,128)} %bitcast.1, ...), custom_call_target="tpu_custom_call" | custom-call | tf_op jit(solution)/shard_map/pallas_call | solution.py:478
  188.0 2.3 %copy.11 = bf16[128,4096]{1,0:T(8,128)(2,1)} copy(bf16[128,4096]{1,0:T(8,128)(2,1)} %shard_map.91) | data formatting | bytes 2097152

commit v4 on v3

--- a/solution.py
+++ b/solution.py
@@ -118,7 +118,7 @@
         send(piece(j, c, r), j, c, r, up_send, {"head": lax.rem(me + 1, peers)}).wait_recv()
 
     own_count = line_chunks * PIECES
-    early = jnp.where(z == ctx - 2, own_count // 2, 0)
+    early = jnp.where(z == ctx - 2, own_count * 3 // 8, 0)
 
     def own_send(i, flag, sem, target, wait=False):
         c, r = line_chunk(lax.div(i, PIECES)), lax.rem(i, PIECES)

time: 190 us -> 186 us (0.979)
  Pallas kernels: 187 us -> 183 us
    pallas_call x1, Pallas kernels: 187 us -> 183 us  [shards(): pl.pallas_call(functools.partial(layer, sizes), out_shape=jax.ShapeDtypeS...]
where the time goes in v4:
time: 186 us
  Pallas kernels  183 us (98%)
  local copies, waits for them, and re-layouts  3.58 us (2%)
    pallas_call x1, Pallas kernels, shards(): pl.pallas_call(functools.partial(layer, sizes), out_shape=jax.ShapeDtypeS...  183 us

profile of v4, /device:TPU:27, one launch (start us, length us, event | category | flops | bytes accessed | tf_op | source)
XLA Modules:
  0.0 186.3 jit_solution(2091923531173358974)
XLA Ops:
  0.0 1.3 reshape.7.gain_ref
  1.3 182.7 %shard_map.91 = bf16[128,4096]{1,0:T(8,128)(2,1)} custom-call(bf16[512,2048]{1,0:T(8,128)(2,1)} %x_ref.1, bf16[512,2048]{1,0:T(8,128)(2,1)} %gate_ref.1, bf16[512,512]{1,0:T(8,128)(2,1)} %bm_ref.1, bf16[512,512]{1,0:T(8,128)(2,1)} %cm_ref.1, f32[32,512]{1,0:T(8,128)} %step_ref.1, f32[32,512]{1,0:T(8,128)} %dec_ref.1, f32[1,32]{1,0:T(1,128)} %bitcast.1, ...), custom_call_target="tpu_custom_call" | custom-call | tf_op jit(solution)/shard_map/pallas_call | solution.py:478
  184.0 2.3 %copy.11 = bf16[128,4096]{1,0:T(8,128)(2,1)} copy(bf16[128,4096]{1,0:T(8,128)(2,1)} %shard_map.91) | data formatting | bytes 2097152
